TPU v7x, 256 devices: a whole 4x4x8 slice. The times are simulated.
256 devices in a mesh: leaf: 64 (over x, z, core), rhs: 4 (over y).
Axes of the slice: x: 4, y: 4, z: 8, core: 2. Of those that a mesh axis runs over, the one named last changes fastest.
Arguments:
- fields: bfloat16 [131072, 1024], P('leaf', 'rhs'), may hold values from -6 to 6
- owner: int32 [131072, 1], P('leaf'), may hold values from 0 to 63; in each aligned block of 2048 rows (0 to 2047, 2048 to 4095, ...) at most 64 rows name the same one
- source_basis: bfloat16 [131072, 256], P('leaf'), may hold values from -0.125 to 0.125
- field_basis: bfloat16 [131072, 256], P('leaf'), may hold values from -0.375 to 0.375
- transfer: bfloat16 [64, 3, 256, 512], P('leaf', None, 'rhs'), may hold values from -0.25 to 0.25
- near_blocks: bfloat16 [512, 7, 256, 256], P('leaf'), may hold values from -0.25 to 0.25
- near_index: int32 [512, 7], P('leaf'), may hold values from 0 to 7
- near_count: int32 [512], P('leaf'), may hold values from 1 to 7
Outputs:
- scattered: bfloat16 [131072, 1024], P('leaf', 'rhs')
Inputs may be any that keep to these rules, and one draw needn't show every extreme that they name: In the rows of one group of 2048 rows at most 64 name one owner; in some group one owner is named by exactly 64. `near_index`: Row-block numbers counted within the same group of 8 row blocks.
All inputs are finite; a program needn't handle non-finite values.
Results may differ from a plain program's by a relative error of at most 0.006.
Values may be sent and summed in bfloat16 or wider, within the bound.
A program may use at most 128 MiB of HBM per device.

v0:
```python
import jax
import jax.numpy as jnp
from jax import lax
from jax.sharding import PartitionSpec as P


def swapped(value, axis, stride):
    return lax.ppermute(value, axis, [(i, i ^ 1 << stride) for i in range(lax.axis_size(axis))])


def slot_numbers(owners_of, n_leaf, capacity):
    onehot = (owners_of[:, None] == jnp.arange(n_leaf, dtype=jnp.int32)[None, :]).astype(jnp.int32)
    before = jnp.cumsum(onehot, axis=0) - onehot
    rank_in = jnp.sum(before * onehot, axis=1)
    return owners_of * capacity + rank_in


def on_device(
    fields, owner, source_basis, field_basis, transfer, near_blocks, near_index, near_count
):
    n_leaf = lax.axis_size("leaf")
    row_count, col_count = fields.shape
    basis_width = source_basis.shape[1]
    capacity = 2 * row_count // n_leaf
    slot_index = slot_numbers(owner[:, 0], n_leaf, capacity)
    block_rows = near_blocks.shape[2]
    block_count, near_slots = near_index.shape
    chosen = fields.reshape(block_count, block_rows, col_count)[near_index]
    keep_mask = jnp.arange(near_slots, dtype=jnp.int32)[None, :] < near_count[:, None]
    chosen = jnp.where(keep_mask[:, :, None, None], chosen, jnp.zeros((), jnp.bfloat16))
    near_term = jnp.einsum(
        "gjab,gjbn->gan", near_blocks, chosen, preferred_element_type=jnp.float32
    ).reshape(row_count, col_count)
    x_slots = jnp.zeros((n_leaf * capacity, col_count), jnp.bfloat16).at[slot_index].set(fields)
    v_slots = (
        jnp.zeros((n_leaf * capacity, basis_width), jnp.bfloat16).at[slot_index].set(source_basis)
    )
    u_slots = (
        jnp.zeros((n_leaf * capacity, basis_width), jnp.bfloat16).at[slot_index].set(field_basis)
    )
    x_three = x_slots.reshape(n_leaf, capacity, col_count)
    v_three = v_slots.reshape(n_leaf, capacity, basis_width)
    coefficients = lax.psum_scatter(
        jnp.einsum("bck,bcn->bkn", v_three, x_three, preferred_element_type=jnp.float32),
        "leaf",
        scatter_dimension=0,
        tiled=True,
    )[0].astype(jnp.bfloat16)
    for level_num in range(transfer.shape[1]):
        partner = swapped(coefficients, "leaf", level_num)
        stacked = jnp.concatenate([coefficients, partner], axis=0)

        def apply_rows(shard_piece, offset, stacked=stacked):
            return jnp.dot(shard_piece, stacked, preferred_element_type=jnp.float32)

        coefficients = apply_rows(
            lax.all_gather(transfer[0, level_num], "rhs", axis=0, tiled=True), jnp.int32(0)
        ).astype(jnp.bfloat16)
    u_three = u_slots.reshape(n_leaf, capacity, basis_width)
    far_slots = (
        jnp.einsum(
            "bck,bkn->bcn",
            u_three,
            lax.all_gather(coefficients[None], "leaf", axis=0, tiled=True),
            preferred_element_type=jnp.float32,
        )
        .astype(jnp.bfloat16)
        .reshape(n_leaf * capacity, col_count)
    )
    far_term = far_slots[slot_index]
    return (far_term.astype(jnp.float32) + near_term).astype(jnp.bfloat16)


def solution(mesh):
    in_specs = (
        P("leaf", "rhs"),
        P("leaf", None),
        P("leaf", None),
        P("leaf", None),
        P("leaf", None, "rhs", None),
        P("leaf", None, None, None),
        P("leaf", None),
        P("leaf"),
    )
    out_specs = P("leaf", "rhs")
    return jax.shard_map(
        on_device, mesh=mesh, in_specs=in_specs, out_specs=out_specs, check_vma=False
    )
```

profile of v0, /device:TPU:5, one launch (start us, length us, event | category | flops | bytes accessed | tf_op | source)
XLA Modules:
  0.0 411.8 jit_solution(9575077675460994863)
XLA Ops:
  6.5 0.0 reduce-scatter.2.cloned.1.call-start
  6.5 0.0 copy-start.2
  6.5 0.8 fusion.17
  7.3 18.1 %reduce-window.6 = s32[64,16,128]{2,1,0:T(8,128)S(1)} reduce-window(s32[64,16,128]{2,1,0:T(8,128)S(1)} %fusion.17, s32[]{:T(128)} %constant.7.clone.1), window={size=1x1x128 pad=0_0x0_0x127_0}, to_apply=%region_0.0 | reduce-window | flops 16646144 | bytes 1048580 | tf_op jit(solution)/shard_map/reduce-window
  25.5 0.2 slice.24
  25.7 0.0 copy-start
  25.7 0.4 copy.14
  26.1 0.2 reduce-window.9
  26.3 0.2 broadcast_add_fusion
  26.5 0.0 copy-done.2
  26.5 0.3 fusion.16
  26.8 10.4 %scatter_custom_fusion.1 = bf16[4096,256]{1,0:T(8,128)(2,1)S(1)} fusion(s32[2048]{0:T(1024)S(1)} %bitcast.75, bf16[2048,256]{1,0:T(8,128)(2,1)} %param.10, bf16[]{:T(256)} %constant.5.clone.1), kind=kCustom, calls=%fused_computation.20 | custom fusion | bytes 2097664 | tf_op jit(solution)/shard_map/scatter | solution.py:36
  37.2 0.0 copy-done
  37.2 10.9 %scatter_custom_fusion.2 = bf16[4096,256]{1,0:T(8,128)(2,1)} fusion(s32[2048]{0:T(1024)S(1)} %bitcast.76, bf16[2048,256]{1,0:T(8,128)(2,1)S(1)} %copy-done, bf16[]{:T(256)} %constant.5.clone.1), kind=kCustom, calls=%fused_computation.18 | custom fusion | bytes 2097154 | tf_op jit(solution)/shard_map/scatter | solution.py:34
  48.1 9.7 %fusion.35 = f32[64,256,256]{2,1,0:T(8,128)} fusion(bf16[64,64,256]{2,1,0:T(8,128)(2,1)S(1)} %bitcast.66, bf16[64,64,256]{2,1,0:T(8,128)(2,1)} %bitcast.67), kind=kOutput, calls=%fused_computation.55 | convolution fusion | flops 536870912 | bytes 20971520 | tf_op jit(solution)/shard_map/bck,bcn->bkn/dot_general | solution.py:44
  57.8 0.0 copy-start.1
  57.8 0.0 reduce-scatter.2.cloned.1.call-update
  57.8 0.0 all-gather.6.cloned.1.call-start
  57.9 187.9 %reduce-scatter.2.cloned.1.call-done = f32[1,256,256]{2,1,0:T(8,128)} async-done(((f32[64,256,256]{2,1,0:T(8,128)}), f32[1,256,256]{2,1,0:T(8,128)}) %reduce-scatter.2.cloned.1.call-update) | async-done | bytes 262160 | tf_op jit(solution)/shard_map/reduce_scatter | solution.py:43
  245.8 1.0 convert_bitcast_fusion
  246.8 4.8 %collective-permute-start = (bf16[256,256]{1,0:T(8,128)(2,1)S(1)}, bf16[256,256]{1,0:T(8,128)(2,1)S(1)}, u32[]{:S(2)}, u32[]{:S(2)}) collective-permute-start(bf16[256,256]{1,0:T(8,128)(2,1)S(1)} %convert_bitcast_fusion), channel_id=1, source_target_pairs={{0,4},{4,0},{8,12},{12,8},{16,20},{20,16},{24,28},{28,24},{32,36},... | collective-permute-start | bytes 393224 | tf_op jit(solution)/shard_map/ppermute | solution.py:8
  251.6 0.0 copy-done.1
  251.6 9.9 %all-gather = bf16[1,1,256,512]{3,2,1,0:T(8,128)(2,1)S(1)} all-gather(bf16[1,1,64,512]{3,2,1,0:T(8,128)(2,1)S(1)} %get-tuple-element.6), channel_id=2, replica_groups=mesh['leaf'=64,'rhs'=4] {'rhs'}, dimensions={2}, use_global_device_ids=true | all-gather | bytes 327680 | tf_op jit(solution)/shard_map/all_gather | solution.py:57
  261.5 0.0 collective-permute-done
  261.5 0.2 fusion.6
  261.8 0.8 collective-permute-start.1
  262.6 9.4 %all-gather.1 = bf16[1,1,256,512]{3,2,1,0:T(8,128)(2,1)S(1)} all-gather(bf16[1,1,64,512]{3,2,1,0:T(8,128)(2,1)S(1)} %get-tuple-element.7), channel_id=3, replica_groups=mesh['leaf'=64,'rhs'=4] {'rhs'}, dimensions={2}, use_global_device_ids=true | all-gather | bytes 327680 | tf_op jit(solution)/shard_map/all_gather | solution.py:57
  271.9 0.0 copy-start.3
  272.0 0.0 collective-permute-done.1
  272.0 0.2 fusion.7
  272.2 2.6 collective-permute-start.2
  274.8 9.5 %all-gather.2 = bf16[1,1,256,512]{3,2,1,0:T(8,128)(2,1)S(1)} all-gather(bf16[1,1,64,512]{3,2,1,0:T(8,128)(2,1)S(1)} %get-tuple-element.5), channel_id=4, replica_groups=mesh['leaf'=64,'rhs'=4] {'rhs'}, dimensions={2}, use_global_device_ids=true | all-gather | bytes 327680 | tf_op jit(solution)/shard_map/all_gather | solution.py:57
  284.3 0.0 collective-permute-done.2
  284.3 0.9 fusion.5
  285.3 0.0 all-gather.6.cloned.1.call-update
  285.3 11.2 %scatter_custom_fusion = bf16[4096,256]{1,0:T(8,128)(2,1)} fusion(s32[2048]{0:T(1024)S(1)} %bitcast.77, bf16[2048,256]{1,0:T(8,128)(2,1)} %param.11, bf16[]{:T(256)} %constant.5.clone.1), kind=kCustom, calls=%fused_computation.22 | custom fusion | bytes 2097664 | tf_op jit(solution)/shard_map/scatter | solution.py:39
  296.5 0.0 copy-done.3
  296.5 0.1 reshape.74
  296.6 0.0 copy-start.4
  296.6 5.3 %gather_fusion.1 = bf16[56,256,256]{2,1,0:T(8,128)(2,1)} fusion(bf16[8,256,256]{2,1,0:T(8,128)(2,1)S(1)} %bitcast.64, s32[1024]{0:T(1024)S(1)} %pad_clamp_fusion), kind=kCustom, calls=%fused_computation.1 | custom fusion | bytes 14680288 | tf_op jit(solution)/shard_map/gather | solution.py:28
  301.9 0.0 copy-done.4
  301.9 0.1 iota_compare_fusion.2
  302.0 8.8 %fusion = f32[8,256,256,1]{1,2,3,0:T(8,128)} fusion(bf16[8,7,256,256]{3,2,1,0:T(8,128)(2,1)} %param.13, bf16[8,7,256,256]{3,2,1,0:T(8,128)(2,1)} %bitcast.68, pred[8,7]{1,0:T(8,128)(4,1)S(1)} %iota_compare_fusion.2), kind=kOutput, calls=%fused_computation.5 | convolution fusion | flops 1882718208 | bytes 16777272 | tf_op jit(solution)/shard_map/gjab,gjbn->gan/dot_general | solution.py:31
  310.8 66.4 %all-gather.6.cloned.1.call-done = bf16[16384,256]{0,1:T(8,128)(2,1)} async-done(((bf16[256,256]{0,1:T(8,128)(2,1)}), bf16[16384,256]{0,1:T(8,128)(2,1)}) %all-gather.6.cloned.1.call-update) | async-done | bytes 8388624 | tf_op jit(solution)/shard_map/all_gather | solution.py:64
  377.1 11.9 %copy.15 = bf16[16384,256]{1,0:T(8,128)(2,1)} copy(bf16[16384,256]{0,1:T(8,128)(2,1)} %all-gather.6.cloned.1.call-done) | data formatting | bytes 16777216 | tf_op jit(solution)/shard_map/all_gather | solution.py:64
  389.0 5.6 %convolution_convert_fusion = bf16[64,64,256]{2,1,0:T(8,128)(2,1)S(1)} fusion(bf16[64,64,256]{2,1,0:T(8,128)(2,1)} %bitcast.65, bf16[64,256,256]{2,1,0:T(8,128)(2,1)} %bitcast.63), kind=kOutput, calls=%fused_computation.11 | convolution fusion | flops 537919488 | bytes 12582912 | tf_op jit(solution)/shard_map/bck,bkn->bcn/dot_general | solution.py:61
  394.6 7.5 %gather_fusion = bf16[2048,256]{1,0:T(8,128)(2,1)S(1)} fusion(bf16[4096,256]{1,0:T(8,128)(2,1)S(1)} %bitcast.62, s32[2048]{0:T(1024)S(1)} %broadcast_clamp_fusion), kind=kCustom, calls=%fused_computation | custom fusion | bytes 2105344 | tf_op jit(solution)/shard_map/gather | solution.py:70
  402.1 2.8 fusion.4
  (5 shorter events, 0.0 us)
Async XLA Ops:
  6.5 239.3 %reduce-scatter.2.cloned.1.call-start = ((), (), s32[]{:S(2)}) async-start(), calls=%async_computation.1 | async-start | bytes 17039360 | tf_op jit(solution)/shard_map/reduce_scatter | solution.py:43
  6.5 20.0 %copy-start.2 = (s32[2048,1]{0,1:T(1,128)S(1)}, s32[2048,1]{0,1:T(1,128)}, u32[]{:S(2)}) copy-start(s32[2048,1]{0,1:T(1,128)} %param.9) | copy-start | bytes 24580
  25.7 11.5 %copy-start = (bf16[2048,256]{1,0:T(8,128)(2,1)S(1)}, bf16[2048,256]{1,0:T(8,128)(2,1)}, u32[]{:S(2)}) copy-start(bf16[2048,256]{1,0:T(8,128)(2,1)} %param.8) | copy-start | bytes 3145732
  57.8 193.8 %copy-start.1 = (bf16[1,3,64,512]{3,2,1,0:T(8,128)(2,1)S(1)}, bf16[1,3,64,512]{3,2,1,0:T(8,128)(2,1)}, u32[]{:S(2)}) copy-start(bf16[1,3,64,512]{3,2,1,0:T(8,128)(2,1)} %param.12) | copy-start | bytes 589828
  57.8 319.3 %all-gather.6.cloned.1.call-start = ((), (), s32[]{:S(2)}) async-start(), calls=%async_computation.2 | async-start | bytes 8519680 | tf_op jit(solution)/shard_map/all_gather | solution.py:64
  246.8 14.7 %collective-permute-start = (bf16[256,256]{1,0:T(8,128)(2,1)S(1)}, bf16[256,256]{1,0:T(8,128)(2,1)S(1)}, u32[]{:S(2)}, u32[]{:S(2)}) collective-permute-start(bf16[256,256]{1,0:T(8,128)(2,1)S(1)} %convert_bitcast_fusion), channel_id=1, source_target_pairs={{0,4},{4,0},{8,12},{12,8},{16,20},{20,16},{24,28},{28,24},{32,36},... | collective-permute-start | bytes 393224 | tf_op jit(solution)/shard_map/ppermute | solution.py:8
  261.8 10.2 %collective-permute-start.1 = (bf16[256,256]{1,0:T(8,128)(2,1)S(1)}, bf16[256,256]{1,0:T(8,128)(2,1)S(1)}, u32[]{:S(2)}, u32[]{:S(2)}) collective-permute-start(bf16[256,256]{1,0:T(8,128)(2,1)S(1)} %fusion.6), channel_id=1, source_target_pairs={{0,8},{4,12},{8,0},{12,4},{16,24},{20,28},{24,16},{28,20},{32,40},... | collective-permute-start | bytes 393224 | tf_op jit(solution)/shard_map/ppermute | solution.py:8
  271.9 24.6 %copy-start.3 = (s32[8,7]{1,0:T(8,128)S(1)}, s32[8,7]{1,0:T(8,128)}, u32[]{:S(2)}) copy-start(s32[8,7]{1,0:T(8,128)} %param.14) | copy-start | bytes 676
  272.2 12.1 %collective-permute-start.2 = (bf16[256,256]{1,0:T(8,128)(2,1)S(1)}, bf16[256,256]{1,0:T(8,128)(2,1)S(1)}, u32[]{:S(2)}, u32[]{:S(2)}) collective-permute-start(bf16[256,256]{1,0:T(8,128)(2,1)S(1)} %fusion.7), channel_id=1, source_target_pairs={{0,16},{4,20},{8,24},{12,28},{16,0},{20,4},{24,8},{28,12},{32,48},... | collective-permute-start | bytes 393224 | tf_op jit(solution)/shard_map/ppermute | solution.py:8
  296.6 5.3 %copy-start.4 = (s32[8]{0:T(128)S(1)}, s32[8]{0:T(128)}, u32[]{:S(2)}) copy-start(s32[8]{0:T(128)} %param.15) | copy-start | bytes 100
Sparse Core Ops, SparseCore 0:
  58.0 187.8 reduce-scatter.1
  285.4 91.6 all-gather.5
where the time goes:
time: 412 us
  waiting for transfers between devices  254 us (62%)
  local copies, waits for them, and re-layouts  57.9 us (14%)
  blocking collectives  28.7 us (7%)
  matrix products  25.5 us (6%)
  other arithmetic  23.5 us (6%)
  between operations  13.5 us (3%)
  starting transfers between devices  8.35 us (2%)
    reduce_scatter x1, waiting for transfers between devices, on_device(): lax.psum_scatter(jnp.einsum('bck,bcn->bkn', v_three, x_three, preferred_e...  188 us
    all_gather x1, waiting for transfers between devices, on_device(): lax.all_gather(coefficients[None], 'leaf', axis=0, tiled=True)  66.4 us
    all_gather x3, blocking collectives, on_device(): lax.all_gather(transfer[0, level_num], 'rhs', axis=0, tiled=True)  28.7 us
    scatter x2, local copies, waits for them, and re-layouts, on_device(): jnp.zeros((n_leaf * capacity, basis_width), jnp.bfloat16).at[slot_index]  21.6 us
    another operation x3, other arithmetic  18.5 us
    all_gather x1, local copies, waits for them, and re-layouts, on_device(): lax.all_gather(coefficients[None], 'leaf', axis=0, tiled=True)  11.9 us
    scatter x1, local copies, waits for them, and re-layouts, on_device(): jnp.zeros((n_leaf * capacity, col_count), jnp.bfloat16).at[slot_index]  10.9 us
    dot_general x1, matrix products, on_device(): jnp.einsum('bck,bcn->bkn', v_three, x_three, preferred_element_type=jnp.f...  9.68 us
  transfers between devices with their start and end apart: 5, of which 2 were waited for; matrix products, arithmetic and copies ran while one was open for 6% of the time, Pallas kernels for 0%

commit v1 on v0

--- a/solution.py
+++ b/solution.py
@@ -1,7 +1,18 @@
+import functools
 import jax
 import jax.numpy as jnp
 from jax import lax
 from jax.sharding import PartitionSpec as P
+
+
+def put_desk(q_in, bus_axis, axis_no):
+    full_n = jax.lax.psum(1, bus_axis)
+    even = list(map(lambda pp: full_n if pp == axis_no else 1, range(q_in.ndim)))
+    r1 = jnp.tile(q_in, even)
+    return jax.lax.all_to_all(r1, bus_axis, split_axis=axis_no, concat_axis=axis_no, tiled=True)
+
+
+ways_use = functools.partial(put_desk, bus_axis="leaf", axis_no=0)
 
 
 def swapped(value, axis, stride):
@@ -61,7 +72,7 @@
         jnp.einsum(
             "bck,bkn->bcn",
             u_three,
-            lax.all_gather(coefficients[None], "leaf", axis=0, tiled=True),
+            ways_use(coefficients[None]),
             preferred_element_type=jnp.float32,
         )
         .astype(jnp.bfloat16)

time: 412 us -> 513 us (1.25)
  waiting for transfers between devices: 254 us -> 348 us
  starting transfers between devices: 8.35 us -> 23.3 us
  local copies, waits for them, and re-layouts: 57.9 us -> 50.3 us
    all_to_all x0 -> x1, waiting for transfers between devices: none -> 160 us  [put_desk(): jax.lax.all_to_all(r1, bus_axis, split_axis=axis_no, concat_axis=axis_no,...]
    all_gather x1 -> x0, waiting for transfers between devices: 66.4 us -> none  [on_device(): lax.all_gather(coefficients[None], 'leaf', axis=0, tiled=True)]
    all_to_all x0 -> x1, starting transfers between devices: none -> 15.2 us  [put_desk(): jax.lax.all_to_all(r1, bus_axis, split_axis=axis_no, concat_axis=axis_no,...]
    all_gather x1 -> x0, local copies, waits for them, and re-layouts: 11.9 us -> none  [on_device(): lax.all_gather(coefficients[None], 'leaf', axis=0, tiled=True)]
  transfers between devices with their start and end apart: 5 -> 5, of which waited for: 2 -> 2; matrix products, arithmetic and copies ran while one was open for 6% -> 5% of each run, Pallas kernels for 0% -> 0%
where the time goes in v1:
time: 513 us; the launch traced here: 512 us
  waiting for transfers between devices  348 us (68%)
  local copies, waits for them, and re-layouts  50.3 us (10%)
  blocking collectives  28.9 us (6%)
  matrix products  24.6 us (5%)
  other arithmetic  23.5 us (5%)
  starting transfers between devices  23.3 us (5%)
  between operations  13.5 us (3%)
    reduce_scatter x1, waiting for transfers between devices, on_device(): lax.psum_scatter(jnp.einsum('bck,bcn->bkn', v_three, x_three, preferred_e...  188 us
    all_to_all x1, waiting for transfers between devices, put_desk(): jax.lax.all_to_all(r1, bus_axis, split_axis=axis_no, concat_axis=axis_no,...  160 us
    all_gather x3, blocking collectives, on_device(): lax.all_gather(transfer[0, level_num], 'rhs', axis=0, tiled=True)  28.9 us
    scatter x2, local copies, waits for them, and re-layouts, on_device(): jnp.zeros((n_leaf * capacity, basis_width), jnp.bfloat16).at[slot_index]  21.7 us
    another operation x3, other arithmetic  18.5 us
    all_to_all x1, starting transfers between devices, put_desk(): jax.lax.all_to_all(r1, bus_axis, split_axis=axis_no, concat_axis=axis_no,...  15.2 us
    scatter x1, local copies, waits for them, and re-layouts, on_device(): jnp.zeros((n_leaf * capacity, col_count), jnp.bfloat16).at[slot_index]  10.9 us
  transfers between devices with their start and end apart: 5, of which 2 were waited for; matrix products, arithmetic and copies ran while one was open for 5% of the time, Pallas kernels for 0%

profile of v1, /device:TPU:5, one launch (start us, length us, event | category | flops | bytes accessed | tf_op | source)
XLA Modules:
  0.0 512.3 jit_solution(13008106623360762228)
XLA Ops:
  6.5 0.0 reduce-scatter.2.cloned.1.call-start
  6.5 0.0 copy-start.2
  6.5 0.8 fusion.17
  7.3 18.1 %reduce-window.6 = s32[64,16,128]{2,1,0:T(8,128)S(1)} reduce-window(s32[64,16,128]{2,1,0:T(8,128)S(1)} %fusion.17, s32[]{:T(128)} %constant.7.clone.1), window={size=1x1x128 pad=0_0x0_0x127_0}, to_apply=%region_0.0 | reduce-window | flops 16646144 | bytes 1048580 | tf_op jit(solution)/shard_map/reduce-window
  25.5 0.2 slice.24
  25.7 0.0 copy-start
  25.7 0.4 copy.12
  26.1 0.2 reduce-window.9
  26.3 0.2 broadcast_add_fusion
  26.5 0.0 copy-done.2
  26.5 0.3 fusion.16
  26.8 10.4 %scatter_custom_fusion.1 = bf16[4096,256]{1,0:T(8,128)(2,1)S(1)} fusion(s32[2048]{0:T(1024)S(1)} %bitcast.73, bf16[2048,256]{1,0:T(8,128)(2,1)} %param.10, bf16[]{:T(256)} %constant.5.clone.1), kind=kCustom, calls=%fused_computation.20 | custom fusion | bytes 2097664 | tf_op jit(solution)/shard_map/scatter | solution.py:47
  37.2 0.0 copy-done
  37.2 10.9 %scatter_custom_fusion.2 = bf16[4096,256]{1,0:T(8,128)(2,1)} fusion(s32[2048]{0:T(1024)S(1)} %bitcast.74, bf16[2048,256]{1,0:T(8,128)(2,1)S(1)} %copy-done, bf16[]{:T(256)} %constant.5.clone.1), kind=kCustom, calls=%fused_computation.18 | custom fusion | bytes 2097154 | tf_op jit(solution)/shard_map/scatter | solution.py:45
  48.1 9.7 %fusion.35 = f32[64,256,256]{2,1,0:T(8,128)} fusion(bf16[64,64,256]{2,1,0:T(8,128)(2,1)S(1)} %bitcast.64, bf16[64,64,256]{2,1,0:T(8,128)(2,1)} %bitcast.65), kind=kOutput, calls=%fused_computation.55 | convolution fusion | flops 536870912 | bytes 20971520 | tf_op jit(solution)/shard_map/bck,bcn->bkn/dot_general | solution.py:55
  57.8 0.0 copy-start.1
  57.8 0.0 reduce-scatter.2.cloned.1.call-update
  57.8 188.0 %reduce-scatter.2.cloned.1.call-done = f32[1,256,256]{2,1,0:T(8,128)} async-done(((f32[64,256,256]{2,1,0:T(8,128)}), f32[1,256,256]{2,1,0:T(8,128)}) %reduce-scatter.2.cloned.1.call-update) | async-done | bytes 262160 | tf_op jit(solution)/shard_map/reduce_scatter | solution.py:54
  245.8 1.0 convert_bitcast_fusion
  246.8 4.8 collective-permute-start
  251.6 0.0 copy-done.1
  251.6 9.9 %all-gather = bf16[1,1,256,512]{3,2,1,0:T(8,128)(2,1)S(1)} all-gather(bf16[1,1,64,512]{3,2,1,0:T(8,128)(2,1)S(1)} %get-tuple-element.6), channel_id=2, replica_groups=mesh['leaf'=64,'rhs'=4] {'rhs'}, dimensions={2}, use_global_device_ids=true | all-gather | bytes 327680 | tf_op jit(solution)/shard_map/all_gather | solution.py:68
  261.5 0.0 collective-permute-done
  261.5 0.2 fusion.5
  261.8 0.8 collective-permute-start.1
  262.6 9.4 %all-gather.1 = bf16[1,1,256,512]{3,2,1,0:T(8,128)(2,1)S(1)} all-gather(bf16[1,1,64,512]{3,2,1,0:T(8,128)(2,1)S(1)} %get-tuple-element.7), channel_id=3, replica_groups=mesh['leaf'=64,'rhs'=4] {'rhs'}, dimensions={2}, use_global_device_ids=true | all-gather | bytes 327680 | tf_op jit(solution)/shard_map/all_gather | solution.py:68
  271.9 0.0 collective-permute-done.1
  272.0 0.2 fusion.6
  272.2 2.5 collective-permute-start.2
  274.7 9.7 %all-gather.2 = bf16[1,1,256,512]{3,2,1,0:T(8,128)(2,1)S(1)} all-gather(bf16[1,1,64,512]{3,2,1,0:T(8,128)(2,1)S(1)} %get-tuple-element.5), channel_id=4, replica_groups=mesh['leaf'=64,'rhs'=4] {'rhs'}, dimensions={2}, use_global_device_ids=true | all-gather | bytes 327680 | tf_op jit(solution)/shard_map/all_gather | solution.py:68
  284.3 0.0 collective-permute-done.2
  284.3 0.2 fusion.7
  284.6 4.2 tile.2
  288.8 15.2 %all-to-all-start = ((bf16[64,256,256]{2,1,0:T(8,128)(2,1)}), bf16[64,256,256]{2,1,0:T(8,128)(2,1)}, u32[]{:S(2)}, u32[]{:S(2)}) async-start(bf16[64,256,256]{2,1,0:T(8,128)(2,1)} %tile.2), calls=%async_computation.1 | async-start | bytes 16777216 | tf_op jit(solution)/shard_map/all_to_all | solution.py:12
  304.0 0.0 copy-start.3
  304.0 11.3 %scatter_custom_fusion = bf16[4096,256]{1,0:T(8,128)(2,1)} fusion(s32[2048]{0:T(1024)S(1)} %bitcast.75, bf16[2048,256]{1,0:T(8,128)(2,1)} %param.11, bf16[]{:T(256)} %constant.5.clone.1), kind=kCustom, calls=%fused_computation.22 | custom fusion | bytes 2097664 | tf_op jit(solution)/shard_map/scatter | solution.py:50
  315.3 0.0 copy-done.3
  315.3 0.1 reshape.77
  315.4 0.0 copy-start.4
  315.4 5.2 %gather_fusion.1 = bf16[56,256,256]{2,1,0:T(8,128)(2,1)} fusion(bf16[8,256,256]{2,1,0:T(8,128)(2,1)S(1)} %bitcast.62, s32[1024]{0:T(1024)S(1)} %pad_clamp_fusion), kind=kCustom, calls=%fused_computation.1 | custom fusion | bytes 14680288 | tf_op jit(solution)/shard_map/gather | solution.py:39
  320.7 0.0 copy-done.4
  320.7 0.1 iota_compare_fusion.2
  320.8 8.6 %fusion = f32[8,256,256,1]{1,2,3,0:T(8,128)} fusion(bf16[8,7,256,256]{3,2,1,0:T(8,128)(2,1)} %param.13, bf16[8,7,256,256]{3,2,1,0:T(8,128)(2,1)} %bitcast.66, pred[8,7]{1,0:T(8,128)(4,1)S(1)} %iota_compare_fusion.2), kind=kOutput, calls=%fused_computation.5 | convolution fusion | flops 1882718208 | bytes 16777272 | tf_op jit(solution)/shard_map/gjab,gjbn->gan/dot_general | solution.py:42
  329.4 160.2 %all-to-all-done = bf16[64,256,256]{2,1,0:T(8,128)(2,1)} async-done(((bf16[64,256,256]{2,1,0:T(8,128)(2,1)}), bf16[64,256,256]{2,1,0:T(8,128)(2,1)}, u32[]{:S(2)}, u32[]{:S(2)}) %all-to-all-start) | async-done | bytes 8388640 | tf_op jit(solution)/shard_map/all_to_all | solution.py:12
  489.6 5.6 %convolution_convert_fusion = bf16[64,64,256]{2,1,0:T(8,128)(2,1)S(1)} fusion(bf16[64,64,256]{2,1,0:T(8,128)(2,1)} %bitcast.63, bf16[64,256,256]{2,1,0:T(8,128)(2,1)} %all-to-all-done), kind=kOutput, calls=%fused_computation.11 | convolution fusion | flops 537919488 | bytes 12582912 | tf_op jit(solution)/shard_map/bck,bkn->bcn/dot_general | solution.py:72
  495.2 7.5 %gather_fusion = bf16[2048,256]{1,0:T(8,128)(2,1)S(1)} fusion(bf16[4096,256]{1,0:T(8,128)(2,1)S(1)} %bitcast.61, s32[2048]{0:T(1024)S(1)} %broadcast_clamp_fusion), kind=kCustom, calls=%fused_computation | custom fusion | bytes 2105344 | tf_op jit(solution)/shard_map/gather | solution.py:81
  502.7 2.8 fusion.4
  (5 shorter events, 0.0 us)
Async XLA Ops:
  6.5 239.3 %reduce-scatter.2.cloned.1.call-start = ((), (), s32[]{:S(2)}) async-start(), calls=%async_computation.2 | async-start | bytes 17039360 | tf_op jit(solution)/shard_map/reduce_scatter | solution.py:54
  6.5 20.0 %copy-start.2 = (s32[2048,1]{0,1:T(1,128)S(1)}, s32[2048,1]{0,1:T(1,128)}, u32[]{:S(2)}) copy-start(s32[2048,1]{0,1:T(1,128)} %param.9) | copy-start | bytes 24580
  25.7 11.5 %copy-start = (bf16[2048,256]{1,0:T(8,128)(2,1)S(1)}, bf16[2048,256]{1,0:T(8,128)(2,1)}, u32[]{:S(2)}) copy-start(bf16[2048,256]{1,0:T(8,128)(2,1)} %param.8) | copy-start | bytes 3145732
  57.8 193.8 %copy-start.1 = (bf16[1,3,64,512]{3,2,1,0:T(8,128)(2,1)S(1)}, bf16[1,3,64,512]{3,2,1,0:T(8,128)(2,1)}, u32[]{:S(2)}) copy-start(bf16[1,3,64,512]{3,2,1,0:T(8,128)(2,1)} %param.12) | copy-start | bytes 589828
  246.8 14.7 %collective-permute-start = (bf16[256,256]{1,0:T(8,128)(2,1)S(1)}, bf16[256,256]{1,0:T(8,128)(2,1)S(1)}, u32[]{:S(2)}, u32[]{:S(2)}) collective-permute-start(bf16[256,256]{1,0:T(8,128)(2,1)S(1)} %convert_bitcast_fusion), channel_id=1, source_target_pairs={{0,4},{4,0},{8,12},{12,8},{16,20},{20,16},{24,28},{28,24},{32,36},... | collective-permute-start | bytes 393224 | tf_op jit(solution)/shard_map/ppermute | solution.py:19
  261.8 10.2 %collective-permute-start.1 = (bf16[256,256]{1,0:T(8,128)(2,1)S(1)}, bf16[256,256]{1,0:T(8,128)(2,1)S(1)}, u32[]{:S(2)}, u32[]{:S(2)}) collective-permute-start(bf16[256,256]{1,0:T(8,128)(2,1)S(1)} %fusion.5), channel_id=1, source_target_pairs={{0,8},{4,12},{8,0},{12,4},{16,24},{20,28},{24,16},{28,20},{32,40},... | collective-permute-start | bytes 393224 | tf_op jit(solution)/shard_map/ppermute | solution.py:19
  272.2 12.1 %collective-permute-start.2 = (bf16[256,256]{1,0:T(8,128)(2,1)S(1)}, bf16[256,256]{1,0:T(8,128)(2,1)S(1)}, u32[]{:S(2)}, u32[]{:S(2)}) collective-permute-start(bf16[256,256]{1,0:T(8,128)(2,1)S(1)} %fusion.6), channel_id=1, source_target_pairs={{0,16},{4,20},{8,24},{12,28},{16,0},{20,4},{24,8},{28,12},{32,48},... | collective-permute-start | bytes 393224 | tf_op jit(solution)/shard_map/ppermute | solution.py:19
  288.8 200.8 %all-to-all-start = ((bf16[64,256,256]{2,1,0:T(8,128)(2,1)}), bf16[64,256,256]{2,1,0:T(8,128)(2,1)}, u32[]{:S(2)}, u32[]{:S(2)}) async-start(bf16[64,256,256]{2,1,0:T(8,128)(2,1)} %tile.2), calls=%async_computation.1 | async-start | bytes 16777216 | tf_op jit(solution)/shard_map/all_to_all | solution.py:12
  304.0 11.3 %copy-start.3 = (s32[8,7]{1,0:T(8,128)S(1)}, s32[8,7]{1,0:T(8,128)}, u32[]{:S(2)}) copy-start(s32[8,7]{1,0:T(8,128)} %param.14) | copy-start | bytes 676
  315.4 5.2 %copy-start.4 = (s32[8]{0:T(128)S(1)}, s32[8]{0:T(128)}, u32[]{:S(2)}) copy-start(s32[8]{0:T(128)} %param.15) | copy-start | bytes 100
Sparse Core Ops, SparseCore 0:
  58.0 187.8 reduce-scatter.1
